TPU v7x, 32 devices: a whole 2x2x4 slice. The times are simulated.
32 devices in a mesh: hor: 4 (over y, core), lat: 8 (over z, x).
Axes of the slice: x: 2, y: 2, z: 4, core: 2. Of those that a mesh axis runs over, the one named last changes fastest.
Arguments:
- window: float32 [4, 69, 64, 128], P('hor', None, 'lat'), may hold values from -6 to 6
- fresh_noise: float32 [69, 64, 128], P(None, 'lat'), may hold values from -6 to 6
- level_index: int32 [4], P('hor'), may hold values from 4 to 63
- plan: float32 [64], replicated, may hold values from 0.07 to 38.42, as said below
- retention: float32 [4, 192], P('hor'), may hold values from 0.12 to 1
- lift_weight: bfloat16 [192, 69], replicated, may hold values from -0.75 to 0.75
- mod_scale: float32 [192], replicated, may hold values from -3 to 3
- mod_shift: float32 [192], replicated, may hold values from -3 to 3
- conv_weight: bfloat16 [3, 192, 576], replicated, may hold values from -0.15625 to 0.15625
- out_weight: bfloat16 [69, 192], replicated, may hold values from -0.4375 to 0.4375
Outputs:
- window_out: float32 [4, 69, 64, 128], P('hor', None, 'lat')
- rolled: float32 [4, 69, 64, 128], P('hor', None, 'lat')
Inputs may be any that keep to these rules, and one draw needn't show every extreme that they name: `plan`: rising from each entry to the next.
All inputs are finite; a program needn't handle non-finite values.
Results may differ from a plain program's by a relative error of at most 0.00064.
Values may be sent and summed in bfloat16 or wider, within the bound.
A program may use at most 64 MiB of HBM per device.

v0:
```python
import jax
import jax.numpy as jnp
from jax import lax
from jax.sharding import PartitionSpec as P

POOL = 4
STEPS = 3


def padded_2(shard, sides, width):
    for axis, dim in sides:
        size, length = (lax.axis_size(axis), shard.shape[dim])
        up = [(i, (i + 1) % size) for i in range(size - 1)]
        down = [(j, i) for i, j in up]
        last = lax.slice_in_dim(shard, length - width, length, axis=dim)
        leading = lax.slice_in_dim(shard, 0, width, axis=dim)
        before = lax.ppermute(last, axis, up)
        after = lax.ppermute(leading, axis, down)
        shard = jnp.concatenate([before, shard, after], axis=dim)
    return shard


def from_behind(value, axis, steps):
    count = lax.axis_size(axis)
    leading, last = (max(0, -steps), min(count, count - steps))
    return lax.ppermute(value, axis, [(source, source + steps) for source in range(leading, last)])


def body(
    window,
    fresh_noise,
    level_index,
    plan,
    retention,
    lift_weight,
    mod_scale,
    mod_shift,
    conv_weight,
    out_weight,
):
    frames, channels, lat_rows, lon_cells = window.shape
    hor_count = lax.axis_size("hor")
    hor_place = lax.axis_index("hor")
    levels = jnp.arange(plan.shape[0], dtype=jnp.int32)
    hidden = conv_weight.shape[1]
    tap_weight = jnp.transpose(conv_weight.reshape(3, hidden, 3, hidden), (0, 2, 1, 3)).reshape(
        3, 3 * hidden, hidden
    )

    def lookup(level_at):
        onehot = (level_at[:, None] == levels[None, :]).astype(jnp.float32)
        return jnp.sum(onehot * plan[None, :], axis=1)

    current = window
    for section in range(STEPS):
        sigma_now = lookup(level_index - section)
        sigma_next = lookup(level_index - section - 1)
        in_scale = 1.0 / jnp.sqrt(sigma_now * sigma_now + 1.0)
        scaled = (current * in_scale[:, None, None, None]).astype(jnp.bfloat16)
        log_sigma = jnp.log(sigma_now)
        scale_mod = 1.0 + log_sigma[:, None] * mod_scale[None, :]
        shift_mod = log_sigma[:, None] * mod_shift[None, :]
        lifted = jnp.einsum(
            "dc,fclw->fdlw", lift_weight, scaled, preferred_element_type=jnp.float32
        )
        features = jax.nn.silu(
            lifted * scale_mod[:, :, None, None] + shift_mod[:, :, None, None]
        ).astype(jnp.bfloat16)
        padded = padded_2(features, (("lat", 2),), 1)
        blocks = features.astype(jnp.float32).reshape(
            frames, hidden, lat_rows // POOL, POOL, lon_cells // POOL, POOL
        )
        pooled = jnp.mean(blocks, axis=(3, 5)).reshape(frames, hidden, -1)

        def run_local(running, packed):
            product = running[0] * packed[0]
            summed = packed[0][:, None] * running[1] + packed[1]
            return ((product, summed), (product, summed))

        ones_rate = jnp.ones((hidden,), jnp.float32)
        zero_state = jnp.zeros(pooled.shape[1:], jnp.float32)
        (prod_all, last_state), (prods, local_states) = lax.scan(
            run_local, (ones_rate, zero_state), (retention, pooled)
        )
        stacked_rate, stacked_state = (
            lax.all_gather(prod_all[None], "hor", axis=0, tiled=True),
            lax.all_gather(last_state[None], "hor", axis=0, tiled=True),
        )
        positions = jnp.arange(hor_count, dtype=jnp.int32)
        between = (positions[None, :] > positions[:, None]) & (positions[None, :] < hor_place)
        span_weight = jnp.prod(
            jnp.where(between[:, :, None], stacked_rate[None, :, :], 1.0), axis=1
        )
        span_weight = jnp.where((positions < hor_place)[:, None], span_weight, 0.0)
        earlier_sum = jnp.einsum(
            "kd,kdx->dx", span_weight, stacked_state, precision=lax.Precision.HIGHEST
        )
        context = local_states + prods[:, :, None] * earlier_sum[None]
        conv_sum = jnp.zeros((frames, hidden, lat_rows, lon_cells), jnp.float32)
        for row_off in range(3):
            taps_out = jnp.einsum(
                "ek,fklw->felw", tap_weight[row_off], padded, preferred_element_type=jnp.float32
            )
            for col_off in range(3):
                tap_rows = taps_out[
                    :, col_off * hidden : (col_off + 1) * hidden, row_off : row_off + lat_rows, :
                ]
                conv_sum = conv_sum + jnp.roll(tap_rows, 1 - col_off, axis=3)
        coarse = context.reshape(frames, hidden, lat_rows // POOL, 1, lon_cells // POOL, 1)
        spread_ctx = jnp.broadcast_to(
            coarse, (frames, hidden, lat_rows // POOL, POOL, lon_cells // POOL, POOL)
        ).reshape(frames, hidden, lat_rows, lon_cells)
        gated_out = jax.nn.silu(features.astype(jnp.float32) + conv_sum + spread_ctx).astype(
            jnp.bfloat16
        )
        outputs = jnp.einsum(
            "cd,fdlw->fclw", out_weight, gated_out, preferred_element_type=jnp.float32
        )
        skip_scale = 1.0 / (sigma_now * sigma_now + 1.0)
        out_scale = sigma_now * in_scale
        denoised = (
            skip_scale[:, None, None, None] * current + out_scale[:, None, None, None] * outputs
        )
        current = denoised + (sigma_next / sigma_now)[:, None, None, None] * (current - denoised)
    arriving = from_behind(current, "hor", -1)
    top_sigma = plan[plan.shape[0] - 1]
    tail_frame = jnp.where(hor_place == hor_count - 1, top_sigma * fresh_noise[None], arriving)
    rolled = jnp.concatenate([current[1:], tail_frame], axis=0)
    return (current, rolled)


def solution(mesh):
    in_specs = (
        P("hor", None, "lat", None),
        P(None, "lat", None),
        P("hor"),
        P(),
        P("hor", None),
        P(),
        P(),
        P(),
        P(),
        P(),
    )
    out_specs = (P("hor", None, "lat", None), P("hor", None, "lat", None))
    return jax.shard_map(body, mesh=mesh, in_specs=in_specs, out_specs=out_specs, check_vma=False)
```

profile of v0, /device:TPU:25, one launch (start us, length us, event | category | flops | bytes accessed | tf_op | source)
XLA Modules:
  0.0 100.6 jit_solution(8722093664541728765)
XLA Ops:
  1.3 1.3 %fusion.69 = (f32[]{:T(128)}, f32[]{:T(128)}, f32[]{:T(128)}, f32[]{:T(128)}) fusion(f32[64]{0:T(128)} %param.13, s32[]{:T(128)} %bitcast.102, s32[]{:T(128)} %bitcast.261, s32[]{:T(128)} %bitcast.9, s32[]{:T(128)} %bitcast.6), kind=kLoop, calls=%fused_computation.125 | loop fusion | flops 764 | bytes 288 | tf_op jit(solution)/shard_map/reduce_sum | solution.py:52
  5.9 1.0 fusion.55
  6.9 1.3 %multiply_add_fusion.3 = (f32[192]{0:T(256)}, f32[192]{0:T(256)S(1)}, f32[192]{0:T(256)}, f32[192]{0:T(256)}, f32[192]{0:T(256)S(1)}, /*index=5*/f32[192]{0:T(256)}) fusion(f32[192]{0:T(256)} %param.16, f32[]{:T(128)} %bitcast.81, f32[]{:T(128)} %bitcast.20, f32[]{:T(128)} %bitcast.55, f32[192]{0:T(256)} %param.17), kind=kLoop, calls=%fused_computation.119 | loop fusion | flops 1728 | bytes 6156 | tf_op jit(solution)/shard_map/add | solution.py:61
  8.6 0.6 fusion.97
  9.3 3.0 %collective-permute-start.1 = (bf16[1,192,1,128]{3,1,2,0:T(8,128)(2,1)}, bf16[1,192,1,128]{3,1,2,0:T(8,128)(2,1)S(1)}, u32[]{:S(2)}, u32[]{:S(2)}) collective-permute-start(bf16[1,192,1,128]{3,1,2,0:T(8,128)(2,1)} %get-tuple-element.121), channel_id=1, source_target_pairs={{1,0},{2,1},{3,2},{4,3},{5,4},{6,5},{7,6},{9,8},{10,9},{11,10},{12... | collective-permute-start | bytes 147464 | tf_op jit(solution)/shard_map/ppermute | solution.py:18
  12.3 2.3 %collective-permute-start = (bf16[1,192,1,128]{3,1,2,0:T(8,128)(2,1)}, bf16[1,192,1,128]{3,1,2,0:T(8,128)(2,1)S(1)}, u32[]{:S(2)}, u32[]{:S(2)}) collective-permute-start(bf16[1,192,1,128]{3,1,2,0:T(8,128)(2,1)} %get-tuple-element.120), channel_id=1, source_target_pairs={{0,1},{1,2},{2,3},{3,4},{4,5},{5,6},{6,7},{8,9},{9,10},{10,11},{11... | collective-permute-start | bytes 147464 | tf_op jit(solution)/shard_map/ppermute | solution.py:17
  15.4 6.8 %all_gather.15 = f32[4,192,64]{1,2,0:T(8,128)S(1)} all-gather(f32[1,192,64]{1,2,0:T(8,128)S(1)} %bitcast_add_fusion.4), channel_id=1, replica_groups=mesh['hor'=4,'lat'=8] {'hor'}, dimensions={0}, use_global_device_ids=true | all-gather | bytes 245760 | tf_op jit(solution)/shard_map/all_gather | solution.py:87
  22.3 5.0 %all-gather = f32[4,1,192]{2,1,0:T(1,128)S(1)} all-gather(f32[1,1,192]{2,1,0:T(1,128)S(1)} %bitcast.278), channel_id=1, replica_groups=mesh['hor'=4,'lat'=8] {'hor'}, dimensions={0}, use_global_device_ids=true | all-gather | bytes 3840 | tf_op jit(solution)/shard_map/all_gather | solution.py:86
  27.5 0.8 copy.71
  41.6 1.7 %multiply_add_fusion.2 = f32[1,69,8,128]{3,1,2,0:T(8,128)S(1)} fusion(f32[1,192,8,128]{3,1,2,0:T(8,128)S(1)} %copy.79, f32[1,192,8,1]{3,1,2,0:T(8,128)S(1)} %get-tuple-element.110, f32[1,192,8,127]{3,1,2,0:T(8,128)S(1)} %get-tuple-element.112, f32[1,576,10,128]{3,1,2,0:T(8,128)S(1)} %convolution_bitcast_fusion.6, ...), kind=kOutput, calls=%fused_computation.78 | convolution fusion | flops 31881216 | bytes 13578252 | tf_op jit(solution)/shard_map/cd,fdlw->fclw/dot_general | solution.py:116
  43.4 0.7 copy-done.4
  44.8 0.6 fusion.96
  46.1 5.9 %all_gather.16 = f32[4,192,64]{1,2,0:T(8,128)S(1)} all-gather(f32[1,192,64]{1,2,0:T(8,128)S(1)} %bitcast_add_fusion.2), channel_id=1, replica_groups=mesh['hor'=4,'lat'=8] {'hor'}, dimensions={0}, use_global_device_ids=true | all-gather | bytes 245760 | tf_op jit(solution)/shard_map/all_gather | solution.py:87
  51.9 3.9 %collective-permute-start.3 = (bf16[1,192,1,128]{3,1,2,0:T(8,128)(2,1)}, bf16[1,192,1,128]{3,1,2,0:T(8,128)(2,1)S(1)}, u32[]{:S(2)}, u32[]{:S(2)}) collective-permute-start(bf16[1,192,1,128]{3,1,2,0:T(8,128)(2,1)} %get-tuple-element.119), channel_id=1, source_target_pairs={{1,0},{2,1},{3,2},{4,3},{5,4},{6,5},{7,6},{9,8},{10,9},{11,10},{12... | collective-permute-start | bytes 147464 | tf_op jit(solution)/shard_map/ppermute | solution.py:18
  55.9 2.1 %collective-permute-start.2 = (bf16[1,192,1,128]{3,1,2,0:T(8,128)(2,1)}, bf16[1,192,1,128]{3,1,2,0:T(8,128)(2,1)S(1)}, u32[]{:S(2)}, u32[]{:S(2)}) collective-permute-start(bf16[1,192,1,128]{3,1,2,0:T(8,128)(2,1)} %get-tuple-element.118), channel_id=1, source_target_pairs={{0,1},{1,2},{2,3},{3,4},{4,5},{5,6},{6,7},{8,9},{9,10},{10,11},{11... | collective-permute-start | bytes 147464 | tf_op jit(solution)/shard_map/ppermute | solution.py:17
  58.0 0.7 fusion.57
  59.5 2.3 %collective-permute-done.2 = bf16[1,192,1,128]{3,1,2,0:T(8,128)(2,1)S(1)} collective-permute-done((bf16[1,192,1,128]{3,1,2,0:T(8,128)(2,1)}, bf16[1,192,1,128]{3,1,2,0:T(8,128)(2,1)S(1)}, u32[]{:S(2)}, u32[]{:S(2)}) %collective-permute-start.2) | collective-permute-done | bytes 49184 | tf_op jit(solution)/shard_map/ppermute | solution.py:17
  65.5 1.7 %multiply_add_fusion.1 = f32[1,69,8,128]{3,1,2,0:T(8,128)S(1)} fusion(f32[1,69,8,128]{3,1,2,0:T(8,128)S(1)} %copy-done.5, f32[1,192,8,128]{3,1,2,0:T(8,128)S(1)} %copy.85, f32[1,192,8,1]{3,1,2,0:T(8,128)S(1)} %get-tuple-element.98, f32[1,192,8,127]{3,1,2,0:T(8,128)S(1)} %get-tuple-element.100, f32[1,576,10,128]{3,1,2,0:T(8,128)S(1)} %convolution_bitcast_fusion.3, ...), kind=kOutput, calls=%fused_computation.76 | convolution fusion | flops 31881216 | bytes 13590540 | tf_op jit(solution)/shard_map/cd,fdlw->fclw/dot_general | solution.py:116
  67.2 0.7 copy-done.2
  68.6 0.6 fusion.95
  69.9 7.2 %all_gather.17 = f32[4,192,64]{1,2,0:T(8,128)S(1)} all-gather(f32[1,192,64]{1,2,0:T(8,128)S(1)} %bitcast_add_fusion), channel_id=1, replica_groups=mesh['hor'=4,'lat'=8] {'hor'}, dimensions={0}, use_global_device_ids=true | all-gather | bytes 245760 | tf_op jit(solution)/shard_map/all_gather | solution.py:87
  77.1 1.9 %collective-permute-start.5 = (bf16[1,192,1,128]{3,1,2,0:T(8,128)(2,1)}, bf16[1,192,1,128]{3,1,2,0:T(8,128)(2,1)S(1)}, u32[]{:S(2)}, u32[]{:S(2)}) collective-permute-start(bf16[1,192,1,128]{3,1,2,0:T(8,128)(2,1)} %get-tuple-element.117), channel_id=1, source_target_pairs={{1,0},{2,1},{3,2},{4,3},{5,4},{6,5},{7,6},{9,8},{10,9},{11,10},{12... | collective-permute-start | bytes 147464 | tf_op jit(solution)/shard_map/ppermute | solution.py:18
  79.0 3.4 %collective-permute-start.4 = (bf16[1,192,1,128]{3,1,2,0:T(8,128)(2,1)}, bf16[1,192,1,128]{3,1,2,0:T(8,128)(2,1)S(1)}, u32[]{:S(2)}, u32[]{:S(2)}) collective-permute-start(bf16[1,192,1,128]{3,1,2,0:T(8,128)(2,1)} %get-tuple-element.116), channel_id=1, source_target_pairs={{0,1},{1,2},{2,3},{3,4},{4,5},{5,6},{6,7},{8,9},{9,10},{10,11},{11... | collective-permute-start | bytes 147464 | tf_op jit(solution)/shard_map/ppermute | solution.py:17
  82.4 0.7 fusion.56
  84.0 1.0 %collective-permute-done.4 = bf16[1,192,1,128]{3,1,2,0:T(8,128)(2,1)S(1)} collective-permute-done((bf16[1,192,1,128]{3,1,2,0:T(8,128)(2,1)}, bf16[1,192,1,128]{3,1,2,0:T(8,128)(2,1)S(1)}, u32[]{:S(2)}, u32[]{:S(2)}) %collective-permute-start.4) | collective-permute-done | bytes 49184 | tf_op jit(solution)/shard_map/ppermute | solution.py:17
  88.7 1.7 %multiply_add_fusion = f32[1,69,8,128]{3,1,2,0:T(8,128)S(1)} fusion(f32[1,69,8,128]{3,1,2,0:T(8,128)S(1)} %copy-done.3, f32[1,192,8,128]{3,1,2,0:T(8,128)S(1)} %copy.90, f32[1,192,8,1]{3,1,2,0:T(8,128)S(1)} %get-tuple-element.86, f32[1,192,8,127]{3,1,2,0:T(8,128)S(1)} %get-tuple-element.88, f32[1,576,10,128]{3,1,2,0:T(8,128)S(1)} %convolution_bitcast_fusion, ...), kind=kOutput, calls=%fused_computation.74 | convolution fusion | flops 31881216 | bytes 13590540 | tf_op jit(solution)/shard_map/cd,fdlw->fclw/dot_general | solution.py:116
  90.4 3.2 %collective-permute-start.6 = (f32[1,69,8,128]{3,1,2,0:T(8,128)S(1)}, f32[1,69,8,128]{3,1,2,0:T(8,128)S(1)}, u32[]{:S(2)}, u32[]{:S(2)}) collective-permute-start(f32[1,69,8,128]{3,1,2,0:T(8,128)S(1)} %multiply_add_fusion), channel_id=1, source_target_pairs={{8,0},{16,8},{24,16},{9,1},{17,9},{25,17},{10,2},{18,10},{26,18},{... | collective-permute-start | bytes 847880 | tf_op jit(solution)/shard_map/ppermute | solution.py:26
  93.6 0.6 slice.286
  94.2 0.8 copy.92
  95.0 4.2 %collective-permute-done.6 = f32[1,69,8,128]{3,1,2,0:T(8,128)S(1)} collective-permute-done((f32[1,69,8,128]{3,1,2,0:T(8,128)S(1)}, f32[1,69,8,128]{3,1,2,0:T(8,128)S(1)}, u32[]{:S(2)}, u32[]{:S(2)}) %collective-permute-start.6) | collective-permute-done | bytes 282656 | tf_op jit(solution)/shard_map/ppermute | solution.py:26
  99.2 0.7 bitcast_select_fusion
  99.9 0.8 copy.93
  (100 shorter events, 18.2 us)
Async XLA Ops:
  0.6 7.5 %copy-start = (bf16[192,69]{0,1:T(8,128)(2,1)S(1)}, bf16[192,69]{0,1:T(8,128)(2,1)}, u32[]{:S(2)}) copy-start(bf16[192,69]{0,1:T(8,128)(2,1)} %param.15) | copy-start | bytes 79492
  8.6 6.8 %copy-start.9 = (f32[1,192]{1,0:T(1,128)S(1)}, f32[1,192]{1,0:T(1,128)}, u32[]{:S(2)}) copy-start(f32[1,192]{1,0:T(1,128)} %param.14) | copy-start | bytes 2308
  8.6 18.9 %copy-start.6 = (bf16[3,192,576]{2,1,0:T(8,128)(2,1)S(1)}, bf16[3,192,576]{2,1,0:T(8,128)(2,1)}, u32[]{:S(2)}) copy-start(bf16[3,192,576]{2,1,0:T(8,128)(2,1)} %param.18) | copy-start | bytes 1990660
  9.3 28.7 %collective-permute-start.1 = (bf16[1,192,1,128]{3,1,2,0:T(8,128)(2,1)}, bf16[1,192,1,128]{3,1,2,0:T(8,128)(2,1)S(1)}, u32[]{:S(2)}, u32[]{:S(2)}) collective-permute-start(bf16[1,192,1,128]{3,1,2,0:T(8,128)(2,1)} %get-tuple-element.121), channel_id=1, source_target_pairs={{1,0},{2,1},{3,2},{4,3},{5,4},{6,5},{7,6},{9,8},{10,9},{11,10},{12... | collective-permute-start | bytes 147464 | tf_op jit(solution)/shard_map/ppermute | solution.py:18
  12.3 25.7 %collective-permute-start = (bf16[1,192,1,128]{3,1,2,0:T(8,128)(2,1)}, bf16[1,192,1,128]{3,1,2,0:T(8,128)(2,1)S(1)}, u32[]{:S(2)}, u32[]{:S(2)}) collective-permute-start(bf16[1,192,1,128]{3,1,2,0:T(8,128)(2,1)} %get-tuple-element.120), channel_id=1, source_target_pairs={{0,1},{1,2},{2,3},{3,4},{4,5},{5,6},{6,7},{8,9},{9,10},{10,11},{11... | collective-permute-start | bytes 147464 | tf_op jit(solution)/shard_map/ppermute | solution.py:17
  40.7 1.0 copy-start.1
  40.7 1.0 copy-start.7
  41.6 2.5 %copy-start.12 = (f32[192]{0:T(256)S(1)}, f32[192]{0:T(256)}, u32[]{:S(2)}) copy-start(f32[192]{0:T(256)} %get-tuple-element.124) | copy-start | bytes 2308
  41.6 2.5 %copy-start.13 = (f32[192]{0:T(256)S(1)}, f32[192]{0:T(256)}, u32[]{:S(2)}) copy-start(f32[192]{0:T(256)} %get-tuple-element.128) | copy-start | bytes 2308
  43.4 0.7 copy-start.4
  51.9 7.6 %collective-permute-start.3 = (bf16[1,192,1,128]{3,1,2,0:T(8,128)(2,1)}, bf16[1,192,1,128]{3,1,2,0:T(8,128)(2,1)S(1)}, u32[]{:S(2)}, u32[]{:S(2)}) collective-permute-start(bf16[1,192,1,128]{3,1,2,0:T(8,128)(2,1)} %get-tuple-element.119), channel_id=1, source_target_pairs={{1,0},{2,1},{3,2},{4,3},{5,4},{6,5},{7,6},{9,8},{10,9},{11,10},{12... | collective-permute-start | bytes 147464 | tf_op jit(solution)/shard_map/ppermute | solution.py:18
  55.9 5.9 %collective-permute-start.2 = (bf16[1,192,1,128]{3,1,2,0:T(8,128)(2,1)}, bf16[1,192,1,128]{3,1,2,0:T(8,128)(2,1)S(1)}, u32[]{:S(2)}, u32[]{:S(2)}) collective-permute-start(bf16[1,192,1,128]{3,1,2,0:T(8,128)(2,1)} %get-tuple-element.118), channel_id=1, source_target_pairs={{0,1},{1,2},{2,3},{3,4},{4,5},{5,6},{6,7},{8,9},{9,10},{10,11},{11... | collective-permute-start | bytes 147464 | tf_op jit(solution)/shard_map/ppermute | solution.py:17
  64.5 1.0 copy-start.5
  65.5 2.4 %copy-start.10 = (f32[192]{0:T(256)S(1)}, f32[192]{0:T(256)}, u32[]{:S(2)}) copy-start(f32[192]{0:T(256)} %get-tuple-element.122) | copy-start | bytes 2308
  65.5 2.4 %copy-start.11 = (f32[192]{0:T(256)S(1)}, f32[192]{0:T(256)}, u32[]{:S(2)}) copy-start(f32[192]{0:T(256)} %get-tuple-element.130) | copy-start | bytes 2308
  67.2 0.7 copy-start.2
  77.1 6.8 %collective-permute-start.5 = (bf16[1,192,1,128]{3,1,2,0:T(8,128)(2,1)}, bf16[1,192,1,128]{3,1,2,0:T(8,128)(2,1)S(1)}, u32[]{:S(2)}, u32[]{:S(2)}) collective-permute-start(bf16[1,192,1,128]{3,1,2,0:T(8,128)(2,1)} %get-tuple-element.117), channel_id=1, source_target_pairs={{1,0},{2,1},{3,2},{4,3},{5,4},{6,5},{7,6},{9,8},{10,9},{11,10},{12... | collective-permute-start | bytes 147464 | tf_op jit(solution)/shard_map/ppermute | solution.py:18
  79.0 5.9 %collective-permute-start.4 = (bf16[1,192,1,128]{3,1,2,0:T(8,128)(2,1)}, bf16[1,192,1,128]{3,1,2,0:T(8,128)(2,1)S(1)}, u32[]{:S(2)}, u32[]{:S(2)}) collective-permute-start(bf16[1,192,1,128]{3,1,2,0:T(8,128)(2,1)} %get-tuple-element.116), channel_id=1, source_target_pairs={{0,1},{1,2},{2,3},{3,4},{4,5},{5,6},{6,7},{8,9},{9,10},{10,11},{11... | collective-permute-start | bytes 147464 | tf_op jit(solution)/shard_map/ppermute | solution.py:17
  87.7 1.0 copy-start.3
  88.7 5.0 %copy-start.14 = (f32[64]{0:T(128)S(1)}, f32[64]{0:T(128)}, u32[]{:S(2)}) copy-start(f32[64]{0:T(128)} %param.13) | copy-start | bytes 772
  88.7 10.5 %copy-start.8 = (f32[69,8,128]{2,1,0:T(8,128)S(1)}, f32[69,8,128]{2,1,0:T(8,128)}, u32[]{:S(2)}) copy-start(f32[69,8,128]{2,1,0:T(8,128)} %param.11) | copy-start | bytes 847876
  90.4 8.7 %collective-permute-start.6 = (f32[1,69,8,128]{3,1,2,0:T(8,128)S(1)}, f32[1,69,8,128]{3,1,2,0:T(8,128)S(1)}, u32[]{:S(2)}, u32[]{:S(2)}) collective-permute-start(f32[1,69,8,128]{3,1,2,0:T(8,128)S(1)} %multiply_add_fusion), channel_id=1, source_target_pairs={{8,0},{16,8},{24,16},{9,1},{17,9},{25,17},{10,2},{18,10},{26,18},{... | collective-permute-start | bytes 847880 | tf_op jit(solution)/shard_map/ppermute | solution.py:26
where the time goes:
time: 101 us
  blocking collectives  25 us (25%)
  starting transfers between devices  19.8 us (20%)
  local copies, waits for them, and re-layouts  17.1 us (17%)
  between operations  13.2 us (13%)
  matrix products  11.3 us (11%)
  waiting for transfers between devices  7.48 us (7%)
  other arithmetic  6.91 us (7%)
    all_gather x3, blocking collectives, body(): lax.all_gather(last_state[None], 'hor', axis=0, tiled=True)  19.9 us
    ppermute x3, starting transfers between devices, padded_2(): after = lax.ppermute(leading, axis, down)  8.81 us
    ppermute x3, starting transfers between devices, padded_2(): before = lax.ppermute(last, axis, up)  7.74 us
    dot_general x3, matrix products, body(): jnp.einsum('cd,fdlw->fclw', out_weight, gated_out, preferred_element_type...  5.17 us
    all_gather x1, blocking collectives, body(): lax.all_gather(prod_all[None], 'hor', axis=0, tiled=True)  5.05 us
    slice x18, local copies, waits for them, and re-layouts, body(): conv_sum = conv_sum + jnp.roll(tap_rows, 1 - col_off, axis=3)  4.98 us
    unnamed x34, local copies, waits for them, and re-layouts  4.95 us
    dot_general x9, matrix products, body(): jnp.einsum('ek,fklw->felw', tap_weight[row_off], padded, preferred_elemen...  4.83 us
  transfers between devices with their start and end apart: 7, of which 3 were waited for; matrix products, arithmetic and copies ran while one was open for 8% of the time, Pallas kernels for 0%

commit v1 on v0

v1 whole, which is shorter than its diff:
```python
import functools

import jax
import jax.numpy as jnp
from jax import lax
from jax.experimental import pallas as pl
from jax.experimental.pallas import tpu as pltpu
from jax.sharding import PartitionSpec as P

POOL = 4
STEPS = 3
MESH = pl.DeviceIdType.MESH
F32 = jnp.float32
BF16 = jnp.bfloat16
WIRE = jnp.bfloat16


def dot(a, b):
    return jnp.dot(a, b, preferred_element_type=F32)


def silu(x):
    h = 0.5 * x
    return h + h * jnp.tanh(h)


def kernel(
    rows,
    lon,
    n_hor,
    n_lat,
    lvl,
    plan,
    win,
    ret,
    msc,
    msh,
    liftw,
    convw,
    outw,
    wout,
    arr,
    cur,
    stack,
    acc,
    up,
    coef,
    mods,
    poolm,
    spread,
    ctx,
    hsend,
    hrecv,
    psend,
    precv,
    rrecv,
    h_ssem,
    h_rsem,
    p_ssem,
    p_rsem,
    r_ssem,
    r_rsem,
    f_sem,
):
    hidden, chans = liftw.shape
    half = hidden // 2
    pair = 2 * lon
    n_pairs = rows // 2
    hor = lax.axis_index("hor")
    lat = lax.axis_index("lat")

    barrier = pltpu.get_barrier_semaphore()

    @pl.when(lat > 0)
    def _():
        pl.semaphore_signal(barrier, inc=1, device_id={"lat": lat - 1}, device_id_type=MESH)

    @pl.when(lat < n_lat - 1)
    def _():
        pl.semaphore_signal(barrier, inc=1, device_id={"lat": lat + 1}, device_id_type=MESH)

    for d in range(1, n_hor):
        pl.semaphore_signal(
            barrier, inc=1, device_id={"hor": lax.rem(hor + d, n_hor)}, device_id_type=MESH
        )

    for row in range(rows):
        cur[:, row * lon : (row + 1) * lon] = win[pl.ds(row, chans, stride=rows), :]

    def column(row_ref_value, start, count):
        sub = lax.broadcasted_iota(jnp.int32, (count, hidden), 0) + start
        lane = lax.broadcasted_iota(jnp.int32, (count, hidden), 1)
        return jnp.sum(jnp.where(sub == lane, row_ref_value, 0.0), axis=1, keepdims=True)

    mods[0] = jnp.broadcast_to(column(msc[...], 0, hidden), (hidden, lon))
    mods[1] = jnp.broadcast_to(column(msh[...], 0, hidden), (hidden, lon))

    def packed_rate(value):
        lane = lax.broadcasted_iota(jnp.int32, (half, lon), 1)
        lo = jnp.broadcast_to(column(value, 0, half), (half, lon))
        hi = jnp.broadcast_to(column(value, half, half), (half, lon))
        return jnp.where(lane < lon // 2, lo, hi)

    groups = lon // POOL
    for tok in range(rows // POOL):
        for side in range(2):
            k = lax.broadcasted_iota(jnp.int32, (pair, lon), 0)
            n = lax.broadcasted_iota(jnp.int32, (pair, lon), 1)
            want = side * (lon // 2) + tok * groups + lax.shift_right_logical(
                lax.bitwise_and(k, lon - 1), POOL.bit_length() - 1
            )
            poolm[2 * tok + side] = jnp.where(want == n, 1.0 / (POOL * POOL), 0.0).astype(BF16)
    for side in range(2):
        k = lax.broadcasted_iota(jnp.int32, (2 * lon, pair), 0)
        n = lax.broadcasted_iota(jnp.int32, (2 * lon, pair), 1)
        want = side * (lon // 2) + lax.shift_right_logical(n, POOL.bit_length() - 1)
        spread[side] = jnp.where(lax.bitwise_and(k, lon - 1) == want, 1.0, 0.0).astype(BF16)

    def sigma(s, width):
        at = lvl[0] - s
        now = jnp.full((1, width), plan[jnp.maximum(at, 0)], F32)
        after = jnp.full((1, width), plan[jnp.maximum(at - 1, 0)], F32)
        return now, after

    def in_scale_of(now):
        return 1.0 / jnp.sqrt(now * now + 1.0)

    def halo_copy(s, side):
        return pltpu.make_async_remote_copy(
            src_ref=hsend.at[s, side],
            dst_ref=hrecv.at[s, 1 - side],
            send_sem=h_ssem.at[s, side],
            recv_sem=h_rsem.at[s, 1 - side],
            device_id={"lat": lat - 1 if side == 0 else lat + 1},
            device_id_type=MESH,
        )

    def has(side):
        return lat > 0 if side == 0 else lat < n_lat - 1

    def stage_halo(s):
        scale = in_scale_of(sigma(s, lon)[0])
        for side in range(2):
            at = 0 if side == 0 else (rows - 1) * lon
            hsend[s, side, 0:chans, :] = (cur[:, at : at + lon] * scale).astype(BF16)

    def send_halo(s):
        for side in range(2):

            @pl.when(has(side))
            def _():
                halo_copy(s, side).start()

    def pool_copy(s, d):
        return pltpu.make_async_remote_copy(
            src_ref=psend.at[s],
            dst_ref=precv.at[s, d - 1],
            send_sem=p_ssem.at[s, d - 1],
            recv_sem=p_rsem.at[s, d - 1],
            device_id={"hor": hor + d},
            device_id_type=MESH,
        )

    def rate_copy(d):
        return pltpu.make_async_remote_copy(
            src_ref=ret,
            dst_ref=rrecv.at[d - 1],
            send_sem=r_ssem.at[d - 1],
            recv_sem=r_rsem.at[d - 1],
            device_id={"hor": hor + d},
            device_id_type=MESH,
        )

    def lift(scaled, sm, sh):
        return silu(dot(liftw[...], scaled) * sm + sh).astype(F32)

    def place(feat, block):
        at = block * lon
        low = feat.astype(BF16)
        stack[0:hidden, at : at + lon] = pltpu.roll(feat, 1, 1).astype(BF16)
        stack[hidden : 2 * hidden, at : at + lon] = low
        stack[2 * hidden : 3 * hidden, at : at + lon] = pltpu.roll(feat, lon - 1, 1).astype(BF16)

    stage_halo(0)
    n_near = jnp.where(lat > 0, 1, 0) + jnp.where(lat < n_lat - 1, 1, 0)
    pl.semaphore_wait(barrier, n_near + (n_hor - 1))
    send_halo(0)
    for d in range(1, n_hor):

        @pl.when(hor + d < n_hor)
        def _():
            rate_copy(d).start()

    @pl.loop(0, STEPS)
    def _(s):
        now, after = sigma(s, lon)
        scale = in_scale_of(now)
        log_sigma = jnp.log(now)
        sm = 1.0 + log_sigma * mods[0]
        sh = log_sigma * mods[1]
        for p in range(n_pairs):
            scaled = jnp.concatenate(
                [
                    (cur[:, (2 * p + i) * lon : (2 * p + i + 1) * lon] * scale).astype(BF16)
                    for i in range(2)
                ],
                axis=1,
            )
            lifted = dot(liftw[...], scaled)
            for i in range(2):
                place(silu(lifted[:, i * lon : (i + 1) * lon] * sm + sh), 2 * p + i + 1)
        pooled = jnp.zeros((half, lon), F32)
        for p in range(n_pairs):
            tok = 2 * p // POOL
            for side in range(2):
                k0 = hidden + side * half
                feat = stack[k0 : k0 + half, (2 * p + 1) * lon : (2 * p + 3) * lon]
                pooled = pooled + dot(feat, poolm[2 * tok + side])
        psend[s] = pooled.astype(WIRE)
        for d in range(1, n_hor):

            @pl.when(hor + d < n_hor)
            def _():
                pool_copy(s, d).start()

        ctx[...] = pooled
        for p in range(n_pairs):
            total = dot(convw[1], stack[:, (2 * p + 1) * lon : (2 * p + 3) * lon])
            if p > 0:
                total = total + dot(convw[0], stack[:, 2 * p * lon : (2 * p + 2) * lon])
            if p < n_pairs - 1:
                total = total + dot(convw[2], stack[:, (2 * p + 2) * lon : (2 * p + 4) * lon])
            acc[:, p * pair : (p + 1) * pair] = total
        acc[:, lon:pair] += dot(convw[0], stack[:, lon:pair])
        last = (rows - 1) * lon
        acc[:, last - lon : last] += dot(convw[2], stack[:, rows * lon : (rows + 1) * lon])

        for side in range(2):

            @pl.when(has(side))
            def _():
                halo_copy(s, 1 - side).wait_recv()
                feat = silu(dot(liftw[...], hrecv[s, side, 0:chans, :]) * sm + sh)
                block = 0 if side == 0 else rows + 1
                place(feat, block)
                at = 0 if side == 0 else last
                acc[:, at : at + lon] += dot(
                    convw[2 * side], stack[:, block * lon : (block + 1) * lon]
                )

        @pl.when(s == 0)
        def _():
            coef[0] = packed_rate(ret[...])
            for d in range(1, n_hor):

                @pl.when(hor >= d)
                def _():
                    rate_copy(d).wait_recv()
                    if d < n_hor - 1:
                        coef[d] = coef[d - 1] * packed_rate(rrecv[d - 1])

        for d in range(1, n_hor):

            @pl.when(hor >= d)
            def _():
                pool_copy(s, d).wait_recv()
                ctx[...] += coef[d - 1] * precv[s, d - 1].astype(F32)

        total = ctx[...]
        high = total.astype(BF16)
        low = (total - high.astype(F32)).astype(BF16)
        both = jnp.concatenate([high, low], axis=1)
        up[0:half, :] = dot(both, spread[0])
        up[half:hidden, :] = dot(both, spread[1])

        ratio = after / now
        keep = ratio + (1.0 - ratio) / (now * now + 1.0)
        gain = (1.0 - ratio) * (now * scale)
        order = [0, n_pairs - 1] + list(range(1, n_pairs - 1))
        for p in order:
            tok = 2 * p // POOL
            ctx_up = up[:, tok * lon : (tok + 1) * lon]
            gated = []
            for i in range(2):
                at = (2 * p + i) * lon
                feat = stack[hidden : 2 * hidden, at + lon : at + 2 * lon].astype(F32)
                gated.append(silu(feat + acc[:, at : at + lon] + ctx_up).astype(BF16))
            outputs = dot(outw[...], jnp.concatenate(gated, axis=1))
            for i in range(2):
                at = (2 * p + i) * lon
                cur[:, at : at + lon] = (
                    keep * cur[:, at : at + lon] + gain * outputs[:, i * lon : (i + 1) * lon]
                )
            if p == order[1]:

                @pl.when(s < STEPS - 1)
                def _():
                    stage_halo(s + 1)
                    send_halo(s + 1)

    for row in range(rows):
        wout[pl.ds(row, chans, stride=rows), :] = cur[:, row * lon : (row + 1) * lon]
    final = pltpu.make_async_remote_copy(
        src_ref=wout,
        dst_ref=arr,
        send_sem=f_sem.at[0],
        recv_sem=f_sem.at[1],
        device_id={"hor": hor - 1},
        device_id_type=MESH,
    )

    @pl.when(hor > 0)
    def _():
        final.start()

    for d in range(1, n_hor):

        @pl.when(hor + d < n_hor)
        def _():
            rate_copy(d).wait_send()
            for s in range(STEPS):
                pool_copy(s, d).wait_send()

    for s in range(STEPS):
        for side in range(2):

            @pl.when(has(side))
            def _():
                halo_copy(s, side).wait_send()

    @pl.when(hor > 0)
    def _():
        final.wait_send()

    @pl.when(hor < n_hor - 1)
    def _():
        final.wait_recv()


def body(
    n_hor,
    n_lat,
    window,
    fresh_noise,
    level_index,
    plan,
    retention,
    lift_weight,
    mod_scale,
    mod_shift,
    conv_weight,
    out_weight,
):
    frames, chans, rows, lon = window.shape
    hidden = conv_weight.shape[1]
    half = hidden // 2
    cells = rows * lon
    cpad = -(-chans // 16) * 16
    peers = max(1, n_hor - 1)
    vmem = pl.BlockSpec(memory_space=pltpu.VMEM)
    smem = pl.BlockSpec(memory_space=pltpu.SMEM)
    flat = jax.ShapeDtypeStruct((chans * rows, lon), F32)
    dma = pltpu.SemaphoreType.DMA
    current, arriving = pl.pallas_call(
        functools.partial(kernel, rows, lon, n_hor, n_lat),
        out_shape=(flat, flat),
        in_specs=[smem, smem] + [vmem] * 7,
        out_specs=(vmem, vmem),
        scratch_shapes=[
            pltpu.VMEM((chans, cells), F32),
            pltpu.VMEM((3 * hidden, cells + 2 * lon), BF16),
            pltpu.VMEM((hidden, cells), F32),
            pltpu.VMEM((hidden, 2 * lon), F32),
            pltpu.VMEM((peers, half, lon), F32),
            pltpu.VMEM((2, hidden, lon), F32),
            pltpu.VMEM((2 * (rows // POOL), 2 * lon, lon), BF16),
            pltpu.VMEM((2, 2 * lon, 2 * lon), BF16),
            pltpu.VMEM((half, lon), F32),
            pltpu.VMEM((STEPS, 2, cpad, lon), BF16),
            pltpu.VMEM((STEPS, 2, cpad, lon), BF16),
            pltpu.VMEM((STEPS, half, lon), WIRE),
            pltpu.VMEM((STEPS, peers, half, lon), WIRE),
            pltpu.VMEM((peers, 1, hidden), F32),
            dma((STEPS, 2)),
            dma((STEPS, 2)),
            dma((STEPS, peers)),
            dma((STEPS, peers)),
            dma((peers,)),
            dma((peers,)),
            dma((2,)),
        ],
        compiler_params=pltpu.CompilerParams(
            collective_id=0, has_side_effects=True, vmem_limit_bytes=40 * 1024 * 1024
        ),
    )(
        level_index,
        plan,
        window.reshape(chans * rows, lon),
        retention,
        mod_scale.reshape(1, hidden),
        mod_shift.reshape(1, hidden),
        lift_weight,
        conv_weight,
        out_weight,
    )
    shape = (frames, chans, rows, lon)
    top = plan[plan.shape[0] - 1]
    last = lax.axis_index("hor") == n_hor - 1
    rolled = jnp.where(last, top * fresh_noise[None], arriving.reshape(shape))
    return (current.reshape(shape), rolled)


def solution(mesh):
    in_specs = (
        P("hor", None, "lat", None),
        P(None, "lat", None),
        P("hor"),
        P(),
        P("hor", None),
        P(),
        P(),
        P(),
        P(),
        P(),
    )
    out_specs = (P("hor", None, "lat", None), P("hor", None, "lat", None))
    run = functools.partial(body, mesh.shape["hor"], mesh.shape["lat"])
    return jax.shard_map(run, mesh=mesh, in_specs=in_specs, out_specs=out_specs, check_vma=False)
```

time: 101 us -> 30.2 us (0.30)
  the two profiles are of different devices: /device:TPU:25 before, /device:TPU:1 now
where the time goes in v1:
time: 30.2 us; the launch traced here: 29.9 us
  Pallas kernels  22.8 us (75%)
  local copies, waits for them, and re-layouts  4.32 us (14%)
  other arithmetic  1.39 us (5%)
  between operations  1.37 us (5%)
    pallas_call x1, Pallas kernels, body(): pl.pallas_call(functools.partial(kernel, rows, lon, n_hor, n_lat), out_sh...  22.8 us
    unnamed x18, local copies, waits for them, and re-layouts  3.74 us
    select_n x1, other arithmetic, body(): rolled = jnp.where(last, top * fresh_noise[None], arriving.reshape(shape))  1.39 us

profile of v1, /device:TPU:1, one launch (start us, length us, event | category | flops | bytes accessed | tf_op | source)
XLA Modules:
  0.0 29.9 jit_solution(15215045977736348043)
XLA Ops:
  0.6 0.0 copy-start.6
  1.3 0.0 copy-done.6
  1.3 0.6 %slice.3 = f32[1]{0:T(128)} slice(f32[64]{0:T(128)S(1)} %copy-done.6), slice={[63:64]} | slice | bytes 8 | tf_op jit(solution)/shard_map/slice | solution.py:407
  1.9 0.0 copy-start.2
  1.9 0.0 copy-start.3
  1.9 0.0 copy-start.4
  1.9 0.0 copy-start.5
  1.9 0.9 %copy.12.liftw = bf16[192,69]{1,0:T(8,128)(2,1)S(1)} copy(bf16[192,69]{0,1:T(8,128)(2,1)} %param.15) | data formatting | bytes 52992 | tf_op args[5]
  2.8 0.0 copy-done.2
  2.9 0.0 copy-done.3
  2.9 0.0 copy-done.4
  2.9 0.0 copy-done.5
  2.9 0.0 copy-start
  2.9 1.1 %copy-done = bf16[3,192,576]{2,1,0:T(8,128)(2,1)S(1)} copy-done((bf16[3,192,576]{2,1,0:T(8,128)(2,1)S(1)}, bf16[3,192,576]{2,1,0:T(8,128)(2,1)}, u32[]{:S(2)}) %copy-start) | copy-done | bytes 663576
  4.0 0.0 copy-start.1
  4.0 1.0 %copy-done.1 = f32[1,69,8,128]{3,2,1,0:T(8,128)S(1)} copy-done((f32[1,69,8,128]{3,2,1,0:T(8,128)S(1)}, f32[1,69,8,128]{3,2,1,0:T(8,128)}, u32[]{:S(2)}) %copy-start.1) | copy-done | bytes 282648
  5.0 0.0 copy-start.7
  5.0 22.8 %shard_map.113 = (f32[552,128]{1,0:T(8,128)S(1)}, f32[552,128]{1,0:T(8,128)S(1)}) custom-call(s32[1]{0:T(128)S(6)} %copy.14.lvl, f32[64]{0:T(128)S(1)} %copy-done.6, f32[552,128]{1,0:T(8,128)S(1)} %bitcast.11, f32[1,192]{1,0:T(1,128)S(1)} %copy-done.3, f32[1,192]{1,0:T(1,128)S(1)} %bitcast.13, f32[1,192]{1,0:T(1,128)S(1)} %bitcast.14, ...), custom_call_target="tpu_custom_call" | custom-call | tf_op jit(solution)/shard_map/pallas_call | solution.py:364
  27.8 0.0 copy-done.7
  27.8 1.4 %fusion = f32[1,69,8,128]{3,2,1,0:T(8,128)} fusion(f32[552,128]{1,0:T(8,128)S(1)} %get-tuple-element.5, f32[69,8,128]{2,1,0:T(8,128)S(1)} %copy-done.7, f32[]{:T(128)} %bitcast.4, pred[]{:T(512)S(6)} %eq.3), kind=kLoop, calls=%fused_computation.1 | loop fusion | flops 141312 | bytes 847877 | tf_op jit(solution)/shard_map/jit(_where)/select_n | solution.py:409
  29.2 0.7 %copy.15 = f32[1,69,8,128]{3,2,1,0:T(8,128)} copy(f32[1,69,8,128]{3,2,1,0:T(8,128)S(1)} %bitcast.12) | data formatting | bytes 565248
Async XLA Ops:
  0.6 0.7 %copy-start.6 = (f32[64]{0:T(128)S(1)}, f32[64]{0:T(128)}, u32[]{:S(2)}) copy-start(f32[64]{0:T(128)} %plan.1) | copy-start | bytes 772
  1.9 1.0 %copy-start.2 = (bf16[69,192]{1,0:T(8,128)(2,1)S(1)}, bf16[69,192]{1,0:T(8,128)(2,1)}, u32[]{:S(2)}) copy-start(bf16[69,192]{1,0:T(8,128)(2,1)} %outw.1) | copy-start | bytes 79492
  1.9 1.0 %copy-start.3 = (f32[1,192]{1,0:T(1,128)S(1)}, f32[1,192]{1,0:T(1,128)}, u32[]{:S(2)}) copy-start(f32[1,192]{1,0:T(1,128)} %ret.1) | copy-start | bytes 2308
  1.9 1.0 %copy-start.4 = (f32[192]{0:T(256)S(1)}, f32[192]{0:T(256)}, u32[]{:S(2)}) copy-start(f32[192]{0:T(256)} %param.16) | copy-start | bytes 2308
  1.9 1.0 %copy-start.5 = (f32[192]{0:T(256)S(1)}, f32[192]{0:T(256)}, u32[]{:S(2)}) copy-start(f32[192]{0:T(256)} %param.17) | copy-start | bytes 2308
  2.9 1.1 %copy-start = (bf16[3,192,576]{2,1,0:T(8,128)(2,1)S(1)}, bf16[3,192,576]{2,1,0:T(8,128)(2,1)}, u32[]{:S(2)}) copy-start(bf16[3,192,576]{2,1,0:T(8,128)(2,1)} %convw.1) | copy-start | bytes 1990660
  4.0 1.0 %copy-start.1 = (f32[1,69,8,128]{3,2,1,0:T(8,128)S(1)}, f32[1,69,8,128]{3,2,1,0:T(8,128)}, u32[]{:S(2)}) copy-start(f32[1,69,8,128]{3,2,1,0:T(8,128)} %param.10) | copy-start | bytes 847876
  5.0 22.8 %copy-start.7 = (f32[69,8,128]{2,1,0:T(8,128)S(1)}, f32[69,8,128]{2,1,0:T(8,128)}, u32[]{:S(2)}) copy-start(f32[69,8,128]{2,1,0:T(8,128)} %param.11) | copy-start | bytes 847876

commit v2 on v1

--- a/solution.py
+++ b/solution.py
@@ -31,15 +31,28 @@
     n_lat,
     lvl,
     plan,
+    win_h,
+    fresh_h,
+    ret_h,
+    msc_h,
+    msh_h,
+    lift_h,
+    convw_h,
+    outw_h,
+    wout,
+    arr,
     win,
     ret,
     msc,
     msh,
-    liftw,
+    liftt,
     convw,
     outw,
-    wout,
-    arr,
+    liftw,
+    base_send,
+    base_recv,
+    gain_send,
+    gain_recv,
     cur,
     stack,
     acc,
@@ -60,7 +73,10 @@
     p_rsem,
     r_ssem,
     r_rsem,
+    l_sem,
     f_sem,
+    g_ssem,
+    g_rsem,
 ):
     hidden, chans = liftw.shape
     half = hidden // 2
@@ -84,16 +100,27 @@
             barrier, inc=1, device_id={"hor": lax.rem(hor + d, n_hor)}, device_id_type=MESH
         )
 
-    for row in range(rows):
-        cur[:, row * lon : (row + 1) * lon] = win[pl.ds(row, chans, stride=rows), :]
+    pairs = [(win_h, win), (msc_h, msc), (msh_h, msh), (ret_h, ret), (lift_h, liftt)]
+    pairs += [(convw_h, convw), (outw_h, outw)]
+    loads = [pltpu.make_async_copy(a, b, l_sem.at[i]) for i, (a, b) in enumerate(pairs)]
+    fresh_load = pltpu.make_async_copy(fresh_h, arr, l_sem.at[len(pairs)])
+    for load in loads:
+        load.start()
+
+    @pl.when(hor == n_hor - 1)
+    def _():
+        fresh_load.start()
+
+    for side in range(2):
+
+        @pl.when(jnp.logical_not(lat > 0 if side == 0 else lat < n_lat - 1))
+        def _():
+            hrecv[:, side] = jnp.zeros_like(hrecv[:, side])
 
     def column(row_ref_value, start, count):
         sub = lax.broadcasted_iota(jnp.int32, (count, hidden), 0) + start
         lane = lax.broadcasted_iota(jnp.int32, (count, hidden), 1)
         return jnp.sum(jnp.where(sub == lane, row_ref_value, 0.0), axis=1, keepdims=True)
-
-    mods[0] = jnp.broadcast_to(column(msc[...], 0, hidden), (hidden, lon))
-    mods[1] = jnp.broadcast_to(column(msh[...], 0, hidden), (hidden, lon))
 
     def packed_rate(value):
         lane = lax.broadcasted_iota(jnp.int32, (half, lon), 1)
@@ -138,18 +165,36 @@
     def has(side):
         return lat > 0 if side == 0 else lat < n_lat - 1
 
-    def stage_halo(s):
+    def stage_halo(s, side):
         scale = in_scale_of(sigma(s, lon)[0])
-        for side in range(2):
-            at = 0 if side == 0 else (rows - 1) * lon
-            hsend[s, side, 0:chans, :] = (cur[:, at : at + lon] * scale).astype(BF16)
-
-    def send_halo(s):
-        for side in range(2):
-
-            @pl.when(has(side))
-            def _():
-                halo_copy(s, side).start()
+        at = 0 if side == 0 else (rows - 1) * lon
+        hsend[s, side, 0:chans, :] = (cur[:, at : at + lon] * scale).astype(BF16)
+
+    def send_halo(s, side):
+        @pl.when(has(side))
+        def _():
+            halo_copy(s, side).start()
+
+    base_copy = pltpu.make_async_remote_copy(
+        src_ref=base_send,
+        dst_ref=base_recv,
+        send_sem=f_sem.at[0],
+        recv_sem=f_sem.at[1],
+        device_id={"hor": hor - 1},
+        device_id_type=MESH,
+    )
+    units = [[0], [rows - 1]] + [[r, r + 1] for r in range(1, rows - 1, 2)]
+
+    def gain_copy(u):
+        part = pl.ds(units[u][0] * lon, len(units[u]) * lon)
+        return pltpu.make_async_remote_copy(
+            src_ref=gain_send.at[:, part],
+            dst_ref=gain_recv.at[:, part],
+            send_sem=g_ssem.at[u],
+            recv_sem=g_rsem.at[u],
+            device_id={"hor": hor - 1},
+            device_id_type=MESH,
+        )
 
     def pool_copy(s, d):
         return pltpu.make_async_remote_copy(
@@ -181,21 +226,51 @@
         stack[hidden : 2 * hidden, at : at + lon] = low
         stack[2 * hidden : 3 * hidden, at : at + lon] = pltpu.roll(feat, lon - 1, 1).astype(BF16)
 
-    stage_halo(0)
+    loads[0].wait()
+    for row in range(rows):
+        cur[:, row * lon : (row + 1) * lon] = win[pl.ds(row, chans, stride=rows), :]
+    for side in range(2):
+        stage_halo(0, side)
     n_near = jnp.where(lat > 0, 1, 0) + jnp.where(lat < n_lat - 1, 1, 0)
     pl.semaphore_wait(barrier, n_near + (n_hor - 1))
-    send_halo(0)
+    for side in range(2):
+        send_halo(0, side)
+    for load in loads[1:5]:
+        load.wait()
+    mods[0] = jnp.broadcast_to(column(msc[...], 0, hidden), (hidden, lon))
+    mods[1] = jnp.broadcast_to(column(msh[...], 0, hidden), (hidden, lon))
+    eye = (
+        lax.broadcasted_iota(jnp.int32, (chans, chans), 0)
+        == lax.broadcasted_iota(jnp.int32, (chans, chans), 1)
+    ).astype(F32).astype(BF16)
+    liftw[...] = lax.dot_general(
+        liftt[...], eye, (((0,), (0,)), ((), ())), preferred_element_type=F32
+    ).astype(BF16)
     for d in range(1, n_hor):
 
         @pl.when(hor + d < n_hor)
         def _():
             rate_copy(d).start()
+
+    for load in loads[5:]:
+        load.wait()
 
     @pl.loop(0, STEPS)
     def _(s):
         now, after = sigma(s, lon)
         scale = in_scale_of(now)
         log_sigma = jnp.log(now)
+        ratio = after / now
+        keep = ratio + (1.0 - ratio) / (now * now + 1.0)
+        gain = (1.0 - ratio) * (now * scale)
+
+        @pl.when((s == STEPS - 1) & (hor > 0))
+        def _():
+            for row in range(rows):
+                at = row * lon
+                base_send[:, at : at + lon] = keep * cur[:, at : at + lon]
+            base_copy.start()
+
         sm = 1.0 + log_sigma * mods[0]
         sh = log_sigma * mods[1]
         for p in range(n_pairs):
@@ -240,13 +315,17 @@
             @pl.when(has(side))
             def _():
                 halo_copy(s, 1 - side).wait_recv()
-                feat = silu(dot(liftw[...], hrecv[s, side, 0:chans, :]) * sm + sh)
-                block = 0 if side == 0 else rows + 1
-                place(feat, block)
-                at = 0 if side == 0 else last
-                acc[:, at : at + lon] += dot(
-                    convw[2 * side], stack[:, block * lon : (block + 1) * lon]
-                )
+
+        near = jnp.concatenate([hrecv[s, side, 0:chans, :] for side in range(2)], axis=1)
+        near = dot(liftw[...], near)
+        for side in range(2):
+            feat = silu(near[:, side * lon : (side + 1) * lon] * sm + sh)
+            block = 0 if side == 0 else rows + 1
+            place(jnp.where(has(side), feat, 0.0), block)
+            at = 0 if side == 0 else last
+            acc[:, at : at + lon] += dot(
+                convw[2 * side], stack[:, block * lon : (block + 1) * lon]
+            )
 
         @pl.when(s == 0)
         def _():
@@ -273,45 +352,50 @@
         up[0:half, :] = dot(both, spread[0])
         up[half:hidden, :] = dot(both, spread[1])
 
-        ratio = after / now
-        keep = ratio + (1.0 - ratio) / (now * now + 1.0)
-        gain = (1.0 - ratio) * (now * scale)
-        order = [0, n_pairs - 1] + list(range(1, n_pairs - 1))
-        for p in order:
-            tok = 2 * p // POOL
-            ctx_up = up[:, tok * lon : (tok + 1) * lon]
+        for u, unit in enumerate(units):
             gated = []
-            for i in range(2):
-                at = (2 * p + i) * lon
+            for row in unit:
+                at = row * lon
+                tok = row // POOL
+                ctx_up = up[:, tok * lon : (tok + 1) * lon]
                 feat = stack[hidden : 2 * hidden, at + lon : at + 2 * lon].astype(F32)
                 gated.append(silu(feat + acc[:, at : at + lon] + ctx_up).astype(BF16))
-            outputs = dot(outw[...], jnp.concatenate(gated, axis=1))
-            for i in range(2):
-                at = (2 * p + i) * lon
-                cur[:, at : at + lon] = (
-                    keep * cur[:, at : at + lon] + gain * outputs[:, i * lon : (i + 1) * lon]
-                )
-            if p == order[1]:
+            gated = gated[0] if len(gated) == 1 else jnp.concatenate(gated, axis=1)
+            outputs = dot(outw[...], gated)
+            for i, row in enumerate(unit):
+                at = row * lon
+                step = gain * outputs[:, i * lon : (i + 1) * lon]
+                cur[:, at : at + lon] = keep * cur[:, at : at + lon] + step
+                gain_send[0:chans, at : at + lon] = step.astype(BF16)
+            if u < 2:
 
                 @pl.when(s < STEPS - 1)
                 def _():
-                    stage_halo(s + 1)
-                    send_halo(s + 1)
+                    stage_halo(s + 1, u)
+                    send_halo(s + 1, u)
+
+            @pl.when((s == STEPS - 1) & (hor > 0))
+            def _():
+                gain_copy(u).start()
 
     for row in range(rows):
         wout[pl.ds(row, chans, stride=rows), :] = cur[:, row * lon : (row + 1) * lon]
-    final = pltpu.make_async_remote_copy(
-        src_ref=wout,
-        dst_ref=arr,
-        send_sem=f_sem.at[0],
-        recv_sem=f_sem.at[1],
-        device_id={"hor": hor - 1},
-        device_id_type=MESH,
-    )
-
-    @pl.when(hor > 0)
+
+    @pl.when(hor == n_hor - 1)
     def _():
-        final.start()
+        fresh_load.wait()
+        arr[...] = plan[plan.shape[0] - 1] * arr[...]
+
+    @pl.when(hor < n_hor - 1)
+    def _():
+        base_copy.wait_recv()
+        for u in range(len(units)):
+            gain_copy(u).wait_recv()
+            for row in units[u]:
+                at = row * lon
+                arr[pl.ds(row, chans, stride=rows), :] = base_recv[:, at : at + lon] + gain_recv[
+                    0:chans, at : at + lon
+                ].astype(F32)
 
     for d in range(1, n_hor):
 
@@ -330,11 +414,17 @@
 
     @pl.when(hor > 0)
     def _():
-        final.wait_send()
-
-    @pl.when(hor < n_hor - 1)
-    def _():
-        final.wait_recv()
+        base_copy.wait_send()
+        for u in range(len(units)):
+            gain_copy(u).wait_send()
+
+
+def write(a, b, a_out, b_out, sem):
+    copies = [pltpu.make_async_copy(x, y, sem.at[i]) for i, (x, y) in enumerate([(a, a_out), (b, b_out)])]
+    for copy in copies:
+        copy.start()
+    for copy in copies:
+        copy.wait()
 
 
 def body(
@@ -358,15 +448,28 @@
     cpad = -(-chans // 16) * 16
     peers = max(1, n_hor - 1)
     vmem = pl.BlockSpec(memory_space=pltpu.VMEM)
+    hbm = pl.BlockSpec(memory_space=pltpu.HBM)
     smem = pl.BlockSpec(memory_space=pltpu.SMEM)
     flat = jax.ShapeDtypeStruct((chans * rows, lon), F32)
     dma = pltpu.SemaphoreType.DMA
     current, arriving = pl.pallas_call(
         functools.partial(kernel, rows, lon, n_hor, n_lat),
-        out_shape=(flat, flat),
-        in_specs=[smem, smem] + [vmem] * 7,
+        out_shape=(pltpu.VMEM(flat.shape, F32), pltpu.VMEM(flat.shape, F32)),
+        in_specs=[smem, smem] + [hbm] * 8,
         out_specs=(vmem, vmem),
         scratch_shapes=[
+            pltpu.VMEM((chans * rows, lon), F32),
+            pltpu.VMEM((1, hidden), F32),
+            pltpu.VMEM((1, hidden), F32),
+            pltpu.VMEM((1, hidden), F32),
+            pltpu.VMEM((chans, hidden), BF16),
+            pltpu.VMEM(conv_weight.shape, BF16),
+            pltpu.VMEM((chans, hidden), BF16),
+            pltpu.VMEM((hidden, chans), BF16),
+            pltpu.VMEM((chans, cells), F32),
+            pltpu.VMEM((chans, cells), F32),
+            pltpu.VMEM((cpad, cells), BF16),
+            pltpu.VMEM((cpad, cells), BF16),
             pltpu.VMEM((chans, cells), F32),
             pltpu.VMEM((3 * hidden, cells + 2 * lon), BF16),
             pltpu.VMEM((hidden, cells), F32),
@@ -387,27 +490,36 @@
             dma((STEPS, peers)),
             dma((peers,)),
             dma((peers,)),
+            dma((8,)),
             dma((2,)),
+            dma((rows,)),
+            dma((rows,)),
         ],
         compiler_params=pltpu.CompilerParams(
-            collective_id=0, has_side_effects=True, vmem_limit_bytes=40 * 1024 * 1024
+            collective_id=0, has_side_effects=True, vmem_limit_bytes=66400000
         ),
     )(
         level_index,
         plan,
         window.reshape(chans * rows, lon),
+        fresh_noise.reshape(chans * rows, lon),
         retention,
         mod_scale.reshape(1, hidden),
         mod_shift.reshape(1, hidden),
-        lift_weight,
+        lift_weight.T,
         conv_weight,
         out_weight,
     )
     shape = (frames, chans, rows, lon)
-    top = plan[plan.shape[0] - 1]
-    last = lax.axis_index("hor") == n_hor - 1
-    rolled = jnp.where(last, top * fresh_noise[None], arriving.reshape(shape))
-    return (current.reshape(shape), rolled)
+    current, rolled = pl.pallas_call(
+        write,
+        out_shape=(flat, flat),
+        in_specs=[vmem, vmem],
+        out_specs=(hbm, hbm),
+        scratch_shapes=[dma((2,))],
+        compiler_params=pltpu.CompilerParams(vmem_limit_bytes=4 * 1024 * 1024),
+    )(current, arriving)
+    return (current.reshape(shape), rolled.reshape(shape))
 
 
 def solution(mesh):

time: 30.2 us -> 23.8 us (0.79)
  local copies, waits for them, and re-layouts: 4.32 us -> 0 us
  other arithmetic: 1.39 us -> 0 us
  Pallas kernels: 22.8 us -> 22.4 us
    unnamed x18 -> x0, local copies, waits for them, and re-layouts: 3.74 us -> none
    select_n x1 -> x0, other arithmetic: 1.39 us -> none  [body(): rolled = jnp.where(last, top * fresh_noise[None], arriving.reshape(shape))]
    pallas_call x1, Pallas kernels: 22.8 us -> 21.5 us  [body(): pl.pallas_call(functools.partial(kernel, rows, lon, n_hor, n_lat), out_sh...]
    pallas_call x0 -> x1, Pallas kernels: none -> 0.82 us  [body(): pl.pallas_call(write, out_shape=(flat, flat), in_specs=[vmem, vmem], out_...]
    slice x1 -> x0, local copies, waits for them, and re-layouts: 0.58 us -> none  [body(): top = plan[plan.shape[0] - 1]]
where the time goes in v2:
time: 23.8 us; the launch traced here: 23.7 us
  Pallas kernels  22.4 us (94%)
  between operations  1.29 us (5%)
    pallas_call x1, Pallas kernels, body(): pl.pallas_call(functools.partial(kernel, rows, lon, n_hor, n_lat), out_sh...  21.5 us
    pallas_call x1, Pallas kernels, body(): pl.pallas_call(write, out_shape=(flat, flat), in_specs=[vmem, vmem], out_...  0.82 us

profile of v2, /device:TPU:1, one launch (start us, length us, event | category | flops | bytes accessed | tf_op | source)
XLA Modules:
  0.0 23.7 jit_solution(15932533302831229025)
XLA Ops:
  1.3 21.5 %shard_map.113 = (f32[552,128]{1,0:T(8,128)S(1)}, f32[552,128]{1,0:T(8,128)S(1)}) custom-call(s32[1]{0:T(128)S(6)} %copy.12.lvl, f32[64]{0:T(128)} %plan.1, f32[552,128]{1,0:T(8,128)} %bitcast.7, f32[552,128]{1,0:T(8,128)} %bitcast.8, f32[1,192]{1,0:T(1,128)} %ret_h.1, f32[1,192]{1,0:T(1,128)} %bitcast.10, f32[1,192]{1,0:T(1,128)} %bitcast.11, ...), custom_call_target="tpu_custom_call" | custom-call | tf_op jit(solution)/shard_map/pallas_call | solution.py:455
  22.8 0.8 %shard_map.114 = (f32[552,128]{1,0:T(8,128)}, f32[552,128]{1,0:T(8,128)}) custom-call(f32[552,128]{1,0:T(8,128)S(1)} %get-tuple-element.6.a, f32[552,128]{1,0:T(8,128)S(1)} %get-tuple-element.7.b), custom_call_target="tpu_custom_call" | custom-call | tf_op jit(solution)/shard_map/pallas_call | solution.py:514

commit v3 on v2

--- a/solution.py
+++ b/solution.py
@@ -310,23 +310,6 @@
         last = (rows - 1) * lon
         acc[:, last - lon : last] += dot(convw[2], stack[:, rows * lon : (rows + 1) * lon])
 
-        for side in range(2):
-
-            @pl.when(has(side))
-            def _():
-                halo_copy(s, 1 - side).wait_recv()
-
-        near = jnp.concatenate([hrecv[s, side, 0:chans, :] for side in range(2)], axis=1)
-        near = dot(liftw[...], near)
-        for side in range(2):
-            feat = silu(near[:, side * lon : (side + 1) * lon] * sm + sh)
-            block = 0 if side == 0 else rows + 1
-            place(jnp.where(has(side), feat, 0.0), block)
-            at = 0 if side == 0 else last
-            acc[:, at : at + lon] += dot(
-                convw[2 * side], stack[:, block * lon : (block + 1) * lon]
-            )
-
         @pl.when(s == 0)
         def _():
             coef[0] = packed_rate(ret[...])
@@ -352,7 +335,8 @@
         up[0:half, :] = dot(both, spread[0])
         up[half:hidden, :] = dot(both, spread[1])
 
-        for u, unit in enumerate(units):
+        def finish(u):
+            unit = units[u]
             gated = []
             for row in unit:
                 at = row * lon
@@ -377,6 +361,29 @@
             @pl.when((s == STEPS - 1) & (hor > 0))
             def _():
                 gain_copy(u).start()
+
+        for u in range(2, len(units)):
+            finish(u)
+
+        for side in range(2):
+
+            @pl.when(has(side))
+            def _():
+                halo_copy(s, 1 - side).wait_recv()
+
+        near = jnp.concatenate([hrecv[s, side, 0:chans, :] for side in range(2)], axis=1)
+        near = dot(liftw[...], near)
+        for side in range(2):
+            feat = silu(near[:, side * lon : (side + 1) * lon] * sm + sh)
+            block = 0 if side == 0 else rows + 1
+            place(jnp.where(has(side), feat, 0.0), block)
+            at = 0 if side == 0 else last
+            acc[:, at : at + lon] += dot(
+                convw[2 * side], stack[:, block * lon : (block + 1) * lon]
+            )
+
+        finish(0)
+        finish(1)
 
     for row in range(rows):
         wout[pl.ds(row, chans, stride=rows), :] = cur[:, row * lon : (row + 1) * lon]

time: 23.8 us -> 22.7 us (0.954)
  Pallas kernels: 22.4 us -> 21.3 us
    pallas_call x1, Pallas kernels: 21.5 us -> 20.4 us  [body(): pl.pallas_call(functools.partial(kernel, rows, lon, n_hor, n_lat), out_sh...]
where the time goes in v3:
time: 22.7 us; the launch traced here: 22.5 us
  Pallas kernels  21.3 us (94%)
  between operations  1.29 us (6%)
    pallas_call x1, Pallas kernels, body(): pl.pallas_call(functools.partial(kernel, rows, lon, n_hor, n_lat), out_sh...  20.4 us
    pallas_call x1, Pallas kernels, body(): pl.pallas_call(write, out_shape=(flat, flat), in_specs=[vmem, vmem], out_...  0.82 us

profile of v3, /device:TPU:1, one launch (start us, length us, event | category | flops | bytes accessed | tf_op | source)
XLA Modules:
  0.0 22.5 jit_solution(14435786494445284671)
XLA Ops:
  1.3 20.4 %shard_map.113 = (f32[552,128]{1,0:T(8,128)S(1)}, f32[552,128]{1,0:T(8,128)S(1)}) custom-call(s32[1]{0:T(128)S(6)} %copy.12.lvl, f32[64]{0:T(128)} %plan.1, f32[552,128]{1,0:T(8,128)} %bitcast.7, f32[552,128]{1,0:T(8,128)} %bitcast.8, f32[1,192]{1,0:T(1,128)} %ret_h.1, f32[1,192]{1,0:T(1,128)} %bitcast.10, f32[1,192]{1,0:T(1,128)} %bitcast.11, ...), custom_call_target="tpu_custom_call" | custom-call | tf_op jit(solution)/shard_map/pallas_call | solution.py:462
  21.7 0.8 %shard_map.114 = (f32[552,128]{1,0:T(8,128)}, f32[552,128]{1,0:T(8,128)}) custom-call(f32[552,128]{1,0:T(8,128)S(1)} %get-tuple-element.6.a, f32[552,128]{1,0:T(8,128)S(1)} %get-tuple-element.7.b), custom_call_target="tpu_custom_call" | custom-call | tf_op jit(solution)/shard_map/pallas_call | solution.py:521
